TPU v7x, 256 devices: a whole 4x4x8 slice. The times are simulated.
256 devices in a mesh: dp: 2 (over core), expert: 4 (over x), tensor: 32 (over z, y).
Axes of the slice: x: 4, y: 4, z: 8, core: 2. Of those that a mesh axis runs over, the one named last changes fastest.
Arguments:
- tokens: bfloat16 [1024, 3072], P(('dp', 'expert')), may hold values from -6 to 6
- cotangent: bfloat16 [1024, 3072], P(('dp', 'expert')), may hold values from -6 to 6
- gate_weights: bfloat16 [1024, 2], P(('dp', 'expert')), may hold values from 0.099609375 to 0.8984375
- expert_ids: int32 [1024, 2], P(('dp', 'expert')), may hold values from 0 to 3, all different within a row; in each aligned block of 128 rows (0 to 127, 128 to 255, ...) at most 96 rows name the same one
- w_gate: bfloat16 [4, 3072, 8192], P('expert', 'dp', 'tensor'), may hold values from -0.109375 to 0.109375
- w_up: bfloat16 [4, 3072, 8192], P('expert', 'dp', 'tensor'), may hold values from -0.109375 to 0.109375
- w_down: bfloat16 [4, 3072, 8192], P('expert', 'dp', 'tensor'), may hold values from -0.0625 to 0.0625
Outputs:
- input_grad: bfloat16 [1024, 3072], P(('dp', 'expert'))
- gate_grad: bfloat16 [1024, 2], P(('dp', 'expert'))
- grad_gate: bfloat16 [4, 3072, 8192], P('expert', 'dp', 'tensor')
- grad_up: bfloat16 [4, 3072, 8192], P('expert', 'dp', 'tensor')
- grad_down: bfloat16 [4, 3072, 8192], P('expert', 'dp', 'tensor')
Inputs may be any that keep to these rules, and one draw needn't show every extreme that they name: `expert_ids`: each token names 2 different experts. Among the 128 tokens of one block, no expert is named more than 96 times, and in some blocks one expert is named exactly 96 times.
All inputs are finite; a program needn't handle non-finite values.
Results may differ from a plain program's by a relative error of at most 0.025.
Values may be sent and summed in bfloat16 or wider, within the bound.
No kernel may reach another device: no remote copies, remote signals or barrier semaphores. Data moves between devices by JAX's collectives and lax.ppermute only.
A program may use at most 64 MiB of HBM per device.

v0:
```python
import jax
import jax.numpy as jnp
from jax import lax
from jax.sharding import PartitionSpec as P


def slot_numbers(expert_ids, experts):
    labels = lax.broadcasted_iota(jnp.int32, (1, 1, experts), 2)
    onehot = (expert_ids[:, :, None] == labels).astype(jnp.int32).reshape(-1, experts)
    earlier = jnp.cumsum(onehot, axis=0) - onehot
    return jnp.sum(earlier * onehot, axis=1)


def entry_table(expert_ids, experts, capacity):
    flat_slot = slot_numbers(expert_ids, experts)
    target = expert_ids.reshape(-1) * capacity + flat_slot
    entry_count = expert_ids.shape[0] * expert_ids.shape[1]
    entries = jnp.full((experts * capacity,), entry_count, jnp.int32)
    entries = entries.at[target].set(jnp.arange(entry_count, dtype=jnp.int32))
    return (target, entries)


def fill_buffers(tokens, cotangent, gate_weights, entries):
    model_width = tokens.shape[1]
    zero_row = jnp.zeros((1, model_width), tokens.dtype)
    token_rows = entries // 2
    token_pad = jnp.concatenate([tokens, zero_row], 0)
    grad_pad = jnp.concatenate([cotangent, zero_row], 0)
    weight_pad = jnp.concatenate([gate_weights.reshape(-1), jnp.zeros((2,), gate_weights.dtype)], 0)
    return (token_pad[token_rows], grad_pad[token_rows], weight_pad[entries])


def on_device(tokens, cotangent, gate_weights, expert_ids, w_gate, w_up, w_down):
    experts = lax.axis_size("expert")
    tok_count = tokens.shape[0]
    model_width = tokens.shape[1]
    capacity = tok_count * 3 // experts
    target, entries = entry_table(expert_ids, experts, capacity)
    x_flat, dy_flat, g_flat = fill_buffers(tokens, cotangent, gate_weights, entries)
    x_buf = x_flat.reshape(experts, capacity, model_width)
    dy_buf = dy_flat.reshape(experts, capacity, model_width)
    g_buf = g_flat.reshape(experts, capacity)
    gathered = (
        lax.all_gather(w_gate, "dp", axis=1, tiled=True),
        lax.all_gather(w_up, "dp", axis=1, tiled=True),
        lax.all_gather(w_down, "dp", axis=1, tiled=True),
    )
    gate_full = gathered[0][0]
    up_full = gathered[1][0]
    down_full = gathered[2][0]
    x_in, dy_in, g_in = (
        lax.all_to_all(x_buf, "expert", split_axis=0, concat_axis=0, tiled=True),
        lax.all_to_all(dy_buf, "expert", split_axis=0, concat_axis=0, tiled=True),
        lax.all_to_all(g_buf, "expert", split_axis=0, concat_axis=0, tiled=True),
    )
    rows_x = x_in.reshape(-1, model_width)
    rows_dy = dy_in.reshape(-1, model_width)
    factor = g_in.reshape(-1).astype(jnp.float32)[:, None]
    inner = (((1,), (1,)), ((), ()))
    outer = (((0,), (0,)), ((), ()))
    gate_pre = jnp.dot(rows_x, gate_full, preferred_element_type=jnp.float32)
    up_pre = jnp.dot(rows_x, up_full, preferred_element_type=jnp.float32)
    sigma = jax.nn.sigmoid(gate_pre)
    active = gate_pre * sigma
    hidden = (active * up_pre).astype(jnp.bfloat16)
    back = jnp.dot(rows_dy, down_full, preferred_element_type=jnp.float32)
    slot_gate = jnp.sum(hidden.astype(jnp.float32) * back, axis=1)
    hidden_grad = factor * back
    d_pre_gate = (hidden_grad * up_pre * sigma * (1.0 + gate_pre * (1.0 - sigma))).astype(
        jnp.bfloat16
    )
    d_pre_up = (hidden_grad * active).astype(jnp.bfloat16)
    scaled = (factor * rows_dy.astype(jnp.float32)).astype(jnp.bfloat16)
    slot_input = lax.dot_general(
        d_pre_gate, gate_full, inner, preferred_element_type=jnp.float32
    ) + lax.dot_general(d_pre_up, up_full, inner, preferred_element_type=jnp.float32)
    part_gate = lax.dot_general(rows_x, d_pre_gate, outer, preferred_element_type=jnp.float32)
    part_up = lax.dot_general(rows_x, d_pre_up, outer, preferred_element_type=jnp.float32)
    part_down = lax.dot_general(scaled, hidden, outer, preferred_element_type=jnp.float32)
    slot_input = slot_input.reshape(experts, capacity, model_width)
    slot_gate = slot_gate.reshape(experts, capacity)
    summed = (
        lax.psum_scatter(
            slot_input.astype(jnp.bfloat16), "tensor", scatter_dimension=1, tiled=True
        ).astype(jnp.float32),
        lax.psum_scatter(
            slot_gate.astype(jnp.bfloat16), "tensor", scatter_dimension=1, tiled=True
        ).astype(jnp.float32),
    )
    input_share = summed[0].astype(jnp.bfloat16)
    gate_share = summed[1].astype(jnp.bfloat16)
    joined = (
        lax.all_gather(input_share, "tensor", axis=1, tiled=True),
        lax.all_gather(gate_share, "tensor", axis=1, tiled=True),
    )
    returned = (
        lax.all_to_all(joined[0], "expert", split_axis=0, concat_axis=0, tiled=True),
        lax.all_to_all(joined[1], "expert", split_axis=0, concat_axis=0, tiled=True),
    )
    picked = returned[0].reshape(-1, model_width)[target].reshape(tok_count, 2, model_width)
    input_grad = jnp.sum(picked.astype(jnp.float32), axis=1).astype(jnp.bfloat16)
    gate_grad = returned[1].reshape(-1)[target].reshape(tok_count, 2)
    totals = (
        lax.psum_scatter(
            part_gate[None].astype(jnp.bfloat16), "dp", scatter_dimension=1, tiled=True
        ).astype(jnp.float32),
        lax.psum_scatter(
            part_up[None].astype(jnp.bfloat16), "dp", scatter_dimension=1, tiled=True
        ).astype(jnp.float32),
        lax.psum_scatter(
            part_down[None].astype(jnp.bfloat16), "dp", scatter_dimension=1, tiled=True
        ).astype(jnp.float32),
    )
    return (
        input_grad,
        gate_grad,
        totals[0].astype(jnp.bfloat16),
        totals[1].astype(jnp.bfloat16),
        totals[2].astype(jnp.bfloat16),
    )


def solution(mesh):
    return jax.shard_map(
        on_device,
        mesh=mesh,
        in_specs=(
            P(("dp", "expert"), None),
            P(("dp", "expert"), None),
            P(("dp", "expert"), None),
            P(("dp", "expert"), None),
            P("expert", "dp", "tensor"),
            P("expert", "dp", "tensor"),
            P("expert", "dp", "tensor"),
        ),
        out_specs=(
            P(("dp", "expert"), None),
            P(("dp", "expert"), None),
            P("expert", "dp", "tensor"),
            P("expert", "dp", "tensor"),
            P("expert", "dp", "tensor"),
        ),
        check_vma=False,
    )
```

profile of v0, /device:TPU:8, one launch (start us, length us, event | category | flops | bytes accessed | tf_op | source)
XLA Modules:
  0.0 429.8 jit_solution(11514104356832466018)
XLA Ops:
  14.0 2.8 gather_fusion
  17.4 4.3 all-to-all-start
  21.8 3.6 gather_fusion.2
  26.9 3.6 all-to-all-start.2
  32.6 3.6 gather_fusion.1
  36.1 22.7 %all-to-all-done.2 = bf16[4,96,3072]{2,1,0:T(8,128)(2,1)S(1)} async-done(((bf16[4,96,3072]{2,1,0:T(8,128)(2,1)}), bf16[4,96,3072]{2,1,0:T(8,128)(2,1)S(1)}, u32[]{:S(2)}, u32[]{:S(2)}) %all-to-all-start.2) | async-done | bytes 2359328 | tf_op jit(solution)/shard_map/all_to_all | solution.py:52
  58.8 4.5 %all-to-all-start.1 = ((bf16[4,96,3072]{2,1,0:T(8,128)(2,1)}), bf16[4,96,3072]{2,1,0:T(8,128)(2,1)}, u32[]{:S(2)}, u32[]{:S(2)}) async-start(bf16[4,96,3072]{2,1,0:T(8,128)(2,1)} %bitcast.73), calls=%async_computation.1 | async-start | bytes 4718592 | tf_op jit(solution)/shard_map/all_to_all | solution.py:53
  64.2 2.4 fusion.6
  66.7 2.4 fusion.9
  69.1 15.3 %all-gather.6.cloned.1.call-done = bf16[1,3072,256]{2,1,0:T(8,128)(2,1)} async-done(((bf16[1,1536,256]{2,1,0:T(8,128)(2,1)}), bf16[1,3072,256]{2,1,0:T(8,128)(2,1)}) %all-gather.6.cloned.1.call-update) | async-done | bytes 1572880 | tf_op jit(solution)/shard_map/all_gather | solution.py:46
  84.4 6.3 %all-to-all-done.1 = bf16[4,96,3072]{2,1,0:T(8,128)(2,1)} async-done(((bf16[4,96,3072]{2,1,0:T(8,128)(2,1)}), bf16[4,96,3072]{2,1,0:T(8,128)(2,1)}, u32[]{:S(2)}, u32[]{:S(2)}) %all-to-all-start.1) | async-done | bytes 2359328 | tf_op jit(solution)/shard_map/all_to_all | solution.py:53
  90.7 4.1 multiply_reduce_fusion
  97.0 3.3 copy.43
  102.2 153.1 %all-reduce.7.cloned.1.call-done = bf16[4,96,3072]{2,0,1:T(4,128)(2,1)} async-done(((bf16[4,96,3072]{2,0,1:T(4,128)(2,1)}), bf16[4,96,3072]{2,0,1:T(4,128)(2,1)}) %all-reduce.7.cloned.1.call-update) | async-done | bytes 2359312
  257.0 4.0 fusion.2
  265.6 71.4 %all-reduce.4 = bf16[4,96]{1,0:T(4,128)(2,1)S(1)} all-reduce(bf16[4,96]{1,0:T(4,128)(2,1)S(1)} %convert_element_type.89), channel_id=3, replica_groups=mesh['dp'=2,'expert'=4,'tensor'=32] {'tensor'}, use_global_device_ids=true, to_apply=%region_7.8.clone | all-reduce | flops 384 | bytes 1536
  337.2 42.6 %all-gather = bf16[32,3,4]{2,1,0:T(4,128)(2,1)S(1)} all-gather(bf16[1,3,4]{2,1,0:T(4,128)(2,1)S(1)} %bitcast.80), channel_id=1, replica_groups=mesh['dp'=2,'expert'=4,'tensor'=32] {'tensor'}, dimensions={0}, use_global_device_ids=true | all-gather | bytes 792 | tf_op jit(solution)/shard_map/all_gather | solution.py:94
  380.5 4.3 all-to-all-start.4
  384.8 3.9 copy.44
  390.1 3.6 all-to-all-start.3
  396.6 15.0 %all-to-all-done.3 = bf16[4,96,3072]{2,1,0:T(8,128)(2,1)S(1)} async-done(((bf16[4,96,3072]{2,1,0:T(8,128)(2,1)}), bf16[4,96,3072]{2,1,0:T(8,128)(2,1)S(1)}, u32[]{:S(2)}, u32[]{:S(2)}) %all-to-all-start.3) | async-done | bytes 2359328 | tf_op jit(solution)/shard_map/all_to_all | solution.py:97
  411.6 2.7 gather_fusion.3
  414.3 3.5 reshape.114
  417.8 5.1 %reduce_sum.34 = bf16[128,3072]{1,0:T(8,128)(2,1)} reduce(bf16[128,2,3072]{2,1,0:T(2,128)(2,1)S(1)} %reshape.114, bf16[]{:T(256)} %constant.12.clone.1), dimensions={1}, to_apply=%region_5.6 | reduce | flops 393216 | bytes 2359298 | tf_op jit(solution)/shard_map/reduce_sum | solution.py:101
  (80 shorter events, 26.7 us)
Async XLA Ops:
  7.2 14.6 %copy-start.2 = (bf16[128,3072]{1,0:T(8,128)(2,1)S(1)}, bf16[128,3072]{1,0:T(8,128)(2,1)}, u32[]{:S(2)}) copy-start(bf16[128,3072]{1,0:T(8,128)(2,1)} %param.7) | copy-start | bytes 2359300
  7.2 57.0 %all-gather.10.cloned.1.call-start = ((), (), s32[]{:S(2)}) async-start(), calls=%async_computation.10 | async-start | bytes 2359296 | tf_op jit(solution)/shard_map/all_gather | solution.py:44
  17.4 9.5 %all-to-all-start = ((bf16[4,1,96]{2,1,0:T(2,128)(2,1)}), bf16[4,1,96]{2,1,0:T(2,128)(2,1)S(1)}, u32[]{:S(2)}, u32[]{:S(2)}) async-start(bf16[4,1,96]{2,1,0:T(2,128)(2,1)} %all_to_all.28), calls=%async_computation | async-start | bytes 4096 | tf_op jit(solution)/shard_map/all_to_all | solution.py:54
  26.9 31.8 %all-to-all-start.2 = ((bf16[4,96,3072]{2,1,0:T(8,128)(2,1)}), bf16[4,96,3072]{2,1,0:T(8,128)(2,1)S(1)}, u32[]{:S(2)}, u32[]{:S(2)}) async-start(bf16[4,96,3072]{2,1,0:T(8,128)(2,1)} %bitcast.74), calls=%async_computation.2 | async-start | bytes 4718592 | tf_op jit(solution)/shard_map/all_to_all | solution.py:52
  30.6 36.1 %all-gather.8.cloned.1.call-start = ((), (), s32[]{:S(2)}) async-start(), calls=%async_computation.9 | async-start | bytes 2359296 | tf_op jit(solution)/shard_map/all_gather | solution.py:45
  58.8 32.0 %all-to-all-start.1 = ((bf16[4,96,3072]{2,1,0:T(8,128)(2,1)}), bf16[4,96,3072]{2,1,0:T(8,128)(2,1)}, u32[]{:S(2)}, u32[]{:S(2)}) async-start(bf16[4,96,3072]{2,1,0:T(8,128)(2,1)} %bitcast.73), calls=%async_computation.1 | async-start | bytes 4718592 | tf_op jit(solution)/shard_map/all_to_all | solution.py:53
  63.3 21.1 %all-gather.6.cloned.1.call-start = ((), (), s32[]{:S(2)}) async-start(), calls=%async_computation.8 | async-start | bytes 2359296 | tf_op jit(solution)/shard_map/all_gather | solution.py:46
  64.0 191.3 %all-reduce.7.cloned.1.call-start = ((), (), s32[]{:S(2)}) async-start(), calls=%async_computation.15 | async-start | bytes 4718592
  90.7 4.1 copy-start
  94.8 1.4 copy-start.1
  100.3 0.7 copy-start.3
  100.3 156.7 %copy-start.4 = (bf16[384,256]{0,1:T(8,128)(2,1)S(1)}, bf16[384,256]{0,1:T(8,128)(2,1)}, u32[]{:S(2)}) copy-start(bf16[384,256]{0,1:T(8,128)(2,1)} %get-tuple-element.21) | copy-start | bytes 589828
  100.3 284.5 %all-gather.12.cloned.1.call-start = ((), (), s32[]{:S(2)}) async-start(), calls=%async_computation.11 | async-start | bytes 2433024 | tf_op jit(solution)/shard_map/all_gather | solution.py:93
  256.9 166.0 %reduce-scatter.9.cloned.1.call-start = ((), (), s32[]{:S(2)}) async-start(), calls=%async_computation.14 | async-start | bytes 2359296 | tf_op jit(solution)/shard_map/reduce_scatter | solution.py:110
  261.0 162.0 %reduce-scatter.7.cloned.1.call-start = ((), (), s32[]{:S(2)}) async-start(), calls=%async_computation.13 | async-start | bytes 2359296 | tf_op jit(solution)/shard_map/reduce_scatter | solution.py:107
  263.3 159.6 %reduce-scatter.5.cloned.1.call-start = ((), (), s32[]{:S(2)}) async-start(), calls=%async_computation.12 | async-start | bytes 2359296 | tf_op jit(solution)/shard_map/reduce_scatter | solution.py:104
  380.5 9.6 %all-to-all-start.4 = ((bf16[4,1,96]{2,1,0:T(2,128)(2,1)}), bf16[4,1,96]{2,1,0:T(2,128)(2,1)S(1)}, u32[]{:S(2)}, u32[]{:S(2)}) async-start(bf16[4,1,96]{2,1,0:T(2,128)(2,1)} %copy.47), calls=%async_computation.4 | async-start | bytes 4096 | tf_op jit(solution)/shard_map/all_to_all | solution.py:98
  390.1 21.5 %all-to-all-start.3 = ((bf16[4,96,3072]{2,1,0:T(8,128)(2,1)}), bf16[4,96,3072]{2,1,0:T(8,128)(2,1)S(1)}, u32[]{:S(2)}, u32[]{:S(2)}) async-start(bf16[4,96,3072]{2,1,0:T(8,128)(2,1)} %copy.44), calls=%async_computation.3 | async-start | bytes 4718592 | tf_op jit(solution)/shard_map/all_to_all | solution.py:97
Sparse Core Ops, SparseCore 0:
  9.8 18.0 all-gather.9
  33.2 18.4 all-gather.7
  65.9 18.4 all-gather.5
  100.5 154.8 all-reduce.6
  258.4 75.8 all-gather.11
  337.2 13.1 reduce-scatter.8
  353.4 15.7 reduce-scatter.6
  372.3 15.7 reduce-scatter.4
where the time goes:
time: 431 us; the launch traced here: 430 us
  waiting for transfers between devices  218 us (51%)
  blocking collectives  114 us (26%)
  local copies, waits for them, and re-layouts  36.2 us (8%)
  starting transfers between devices  20.8 us (5%)
  matrix products  19 us (4%)
  between operations  15 us (3%)
  other arithmetic  7.21 us (2%)
    unnamed x9, waiting for transfers between devices  155 us
    unnamed x1, blocking collectives  71.4 us
    all_gather x1, blocking collectives, on_device(): lax.all_gather(gate_share, 'tensor', axis=1, tiled=True)  42.6 us
    all_to_all x1, waiting for transfers between devices, on_device(): lax.all_to_all(x_buf, 'expert', split_axis=0, concat_axis=0, tiled=True)  22.7 us
    all_gather x1, waiting for transfers between devices, on_device(): lax.all_gather(w_down, 'dp', axis=1, tiled=True)  15.3 us
    all_to_all x1, waiting for transfers between devices, on_device(): lax.all_to_all(joined[0], 'expert', split_axis=0, concat_axis=0, tiled=True)  15 us
    gather x3, local copies, waits for them, and re-layouts, fill_buffers(): return (token_pad[token_rows], grad_pad[token_rows], weight_pad[entries])  9.97 us
  transfers between devices with their start and end apart: 13, of which 7 were waited for; matrix products, arithmetic and copies ran while one was open for 12% of the time, Pallas kernels for 0%

commit v1 on v0

--- a/solution.py
+++ b/solution.py
@@ -2,6 +2,14 @@
 import jax.numpy as jnp
 from jax import lax
 from jax.sharding import PartitionSpec as P
+from jax.lax import all_to_all, axis_size
+
+
+def use_lots_all_by_axis(frame):
+    odd = axis_size("tensor")
+    clean = jnp.stack(odd * [frame])
+    current_block = all_to_all(clean, split_axis=0, axis_name="tensor", concat_axis=0)
+    return jnp.concatenate(current_block, axis=1)
 
 
 def slot_numbers(expert_ids, experts):
@@ -91,7 +99,7 @@
     gate_share = summed[1].astype(jnp.bfloat16)
     joined = (
         lax.all_gather(input_share, "tensor", axis=1, tiled=True),
-        lax.all_gather(gate_share, "tensor", axis=1, tiled=True),
+        use_lots_all_by_axis(gate_share),
     )
     returned = (
         lax.all_to_all(joined[0], "expert", split_axis=0, concat_axis=0, tiled=True),

time: 431 us -> 404 us (0.937)
  blocking collectives: 114 us -> 87.4 us
    all_gather x1 -> x0, blocking collectives: 42.6 us -> none  [on_device(): lax.all_gather(gate_share, 'tensor', axis=1, tiled=True)]
    all_to_all x0 -> x1, blocking collectives: none -> 16 us  [use_lots_all_by_axis(): all_to_all(clean, split_axis=0, axis_name='tensor', concat_axis=0)]
where the time goes in v1:
time: 404 us; the launch traced here: 403 us
  waiting for transfers between devices  218 us (54%)
  blocking collectives  87.4 us (22%)
  local copies, waits for them, and re-layouts  36 us (9%)
  starting transfers between devices  21 us (5%)
  matrix products  19 us (5%)
  between operations  15 us (4%)
  other arithmetic  7.21 us (2%)
    unnamed x9, waiting for transfers between devices  155 us
    unnamed x1, blocking collectives  71.4 us
    all_to_all x1, waiting for transfers between devices, on_device(): lax.all_to_all(x_buf, 'expert', split_axis=0, concat_axis=0, tiled=True)  22.7 us
    all_to_all x1, blocking collectives, use_lots_all_by_axis(): all_to_all(clean, split_axis=0, axis_name='tensor', concat_axis=0)  16 us
    all_gather x1, waiting for transfers between devices, on_device(): lax.all_gather(w_down, 'dp', axis=1, tiled=True)  15.3 us
    all_to_all x1, waiting for transfers between devices, on_device(): lax.all_to_all(joined[0], 'expert', split_axis=0, concat_axis=0, tiled=True)  15 us
    gather x3, local copies, waits for them, and re-layouts, fill_buffers(): return (token_pad[token_rows], grad_pad[token_rows], weight_pad[entries])  9.97 us
  transfers between devices with their start and end apart: 13, of which 7 were waited for; matrix products, arithmetic and copies ran while one was open for 12% of the time, Pallas kernels for 0%

profile of v1, /device:TPU:8, one launch (start us, length us, event | category | flops | bytes accessed | tf_op | source)
XLA Modules:
  0.0 403.2 jit_solution(6042005174773656829)
XLA Ops:
  14.0 2.8 gather_fusion
  17.4 4.3 %all-to-all-start = ((bf16[4,1,96]{2,1,0:T(2,128)(2,1)}), bf16[4,1,96]{2,1,0:T(2,128)(2,1)S(1)}, u32[]{:S(2)}, u32[]{:S(2)}) async-start(bf16[4,1,96]{2,1,0:T(2,128)(2,1)} %all_to_all.32), calls=%async_computation | async-start | bytes 4096 | tf_op jit(solution)/shard_map/all_to_all | solution.py:62
  21.8 3.6 gather_fusion.2
  26.9 3.6 all-to-all-start.2
  32.6 3.6 gather_fusion.1
  36.1 22.7 %all-to-all-done.2 = bf16[4,96,3072]{2,1,0:T(8,128)(2,1)S(1)} async-done(((bf16[4,96,3072]{2,1,0:T(8,128)(2,1)}), bf16[4,96,3072]{2,1,0:T(8,128)(2,1)S(1)}, u32[]{:S(2)}, u32[]{:S(2)}) %all-to-all-start.2) | async-done | bytes 2359328 | tf_op jit(solution)/shard_map/all_to_all | solution.py:60
  58.8 4.5 %all-to-all-start.1 = ((bf16[4,96,3072]{2,1,0:T(8,128)(2,1)}), bf16[4,96,3072]{2,1,0:T(8,128)(2,1)}, u32[]{:S(2)}, u32[]{:S(2)}) async-start(bf16[4,96,3072]{2,1,0:T(8,128)(2,1)} %bitcast.68), calls=%async_computation.1 | async-start | bytes 4718592 | tf_op jit(solution)/shard_map/all_to_all | solution.py:61
  64.2 2.4 fusion.6
  66.7 2.4 fusion.9
  69.1 15.3 %all-gather.5.cloned.1.call-done = bf16[1,3072,256]{2,1,0:T(8,128)(2,1)} async-done(((bf16[1,1536,256]{2,1,0:T(8,128)(2,1)}), bf16[1,3072,256]{2,1,0:T(8,128)(2,1)}) %all-gather.5.cloned.1.call-update) | async-done | bytes 1572880 | tf_op jit(solution)/shard_map/all_gather | solution.py:54
  84.4 6.3 %all-to-all-done.1 = bf16[4,96,3072]{2,1,0:T(8,128)(2,1)} async-done(((bf16[4,96,3072]{2,1,0:T(8,128)(2,1)}), bf16[4,96,3072]{2,1,0:T(8,128)(2,1)}, u32[]{:S(2)}, u32[]{:S(2)}) %all-to-all-start.1) | async-done | bytes 2359328 | tf_op jit(solution)/shard_map/all_to_all | solution.py:61
  90.7 4.1 %multiply_reduce_fusion = (bf16[384]{0:T(512)(128)(2,1)S(1)}, bf16[384,256]{0,1:T(8,128)(2,1)}, bf16[384,256]{0,1:T(8,128)(2,1)S(1)}, bf16[384,256]{0,1:T(8,128)(2,1)S(1)}) fusion(f32[384,256]{0,1:T(8,128)S(1)} %fusion.9, f32[384,256]{0,1:T(8,128)S(1)} %fusion.6, f32[384]{0:T(512)S(1)} %reshape.125, bf16[384,3072]{1,0:T(8,128)(2,1)} %bitcast.5, ...), kind=kOutput, calls=%fused_computation.24 | convolution fusion | flops 605847168 | bytes 5310720 | tf_op jit(solution)/shard_map/dot_general | solution.py:74
  97.0 3.3 copy.40
  102.2 153.1 %all-reduce.7.cloned.1.call-done = bf16[4,96,3072]{2,0,1:T(4,128)(2,1)} async-done(((bf16[4,96,3072]{2,0,1:T(4,128)(2,1)}), bf16[4,96,3072]{2,0,1:T(4,128)(2,1)}) %all-reduce.7.cloned.1.call-update) | async-done | bytes 2359312
  257.0 4.0 fusion.2
  265.6 71.4 %all-reduce.4 = bf16[4,96]{1,0:T(4,128)(2,1)S(1)} all-reduce(bf16[4,96]{1,0:T(4,128)(2,1)S(1)} %convert_element_type.89), channel_id=3, replica_groups=mesh['dp'=2,'expert'=4,'tensor'=32] {'tensor'}, use_global_device_ids=true, to_apply=%region_7.8.clone | all-reduce | flops 384 | bytes 1536
  337.1 16.0 %all_to_all.40 = bf16[32,4,3]{2,1,0:T(4,128)(2,1)S(1)} all-to-all(bf16[32,4,3]{2,1,0:T(4,128)(2,1)S(1)} %stack.2), channel_id=1, replica_groups=mesh['dp'=2,'expert'=4,'tensor'=32] {'tensor'}, dimensions={0} | all-to-all | bytes 1536 | tf_op jit(solution)/shard_map/all_to_all | solution.py:11
  353.8 4.2 %all-to-all-start.5 = ((bf16[4,1,96]{2,1,0:T(2,128)(2,1)}), bf16[4,1,96]{2,1,0:T(2,128)(2,1)S(1)}, u32[]{:S(2)}, u32[]{:S(2)}) async-start(bf16[4,1,96]{2,1,0:T(2,128)(2,1)} %all_to_all.33), calls=%async_computation.5 | async-start | bytes 4096 | tf_op jit(solution)/shard_map/all_to_all | solution.py:106
  358.1 3.8 copy.41
  363.4 3.8 all-to-all-start.3
  370.0 15.0 %all-to-all-done.3 = bf16[4,96,3072]{2,1,0:T(8,128)(2,1)S(1)} async-done(((bf16[4,96,3072]{2,1,0:T(8,128)(2,1)}), bf16[4,96,3072]{2,1,0:T(8,128)(2,1)S(1)}, u32[]{:S(2)}, u32[]{:S(2)}) %all-to-all-start.3) | async-done | bytes 2359328 | tf_op jit(solution)/shard_map/all_to_all | solution.py:105
  385.1 2.7 gather_fusion.3
  387.8 3.5 reshape.121
  391.3 5.1 %reduce_sum.34 = bf16[128,3072]{1,0:T(8,128)(2,1)} reduce(bf16[128,2,3072]{2,1,0:T(2,128)(2,1)S(1)} %reshape.121, bf16[]{:T(256)} %constant.12.clone.1), dimensions={1}, to_apply=%region_5.6 | reduce | flops 393216 | bytes 2359298 | tf_op jit(solution)/shard_map/reduce_sum | solution.py:109
  (79 shorter events, 26.6 us)
Async XLA Ops:
  7.2 14.6 %copy-start.2 = (bf16[128,3072]{1,0:T(8,128)(2,1)S(1)}, bf16[128,3072]{1,0:T(8,128)(2,1)}, u32[]{:S(2)}) copy-start(bf16[128,3072]{1,0:T(8,128)(2,1)} %param.7) | copy-start | bytes 2359300
  7.2 57.0 %all-gather.9.cloned.1.call-start = ((), (), s32[]{:S(2)}) async-start(), calls=%async_computation.11 | async-start | bytes 2359296 | tf_op jit(solution)/shard_map/all_gather | solution.py:52
  17.4 9.5 %all-to-all-start = ((bf16[4,1,96]{2,1,0:T(2,128)(2,1)}), bf16[4,1,96]{2,1,0:T(2,128)(2,1)S(1)}, u32[]{:S(2)}, u32[]{:S(2)}) async-start(bf16[4,1,96]{2,1,0:T(2,128)(2,1)} %all_to_all.32), calls=%async_computation | async-start | bytes 4096 | tf_op jit(solution)/shard_map/all_to_all | solution.py:62
  26.9 31.8 %all-to-all-start.2 = ((bf16[4,96,3072]{2,1,0:T(8,128)(2,1)}), bf16[4,96,3072]{2,1,0:T(8,128)(2,1)S(1)}, u32[]{:S(2)}, u32[]{:S(2)}) async-start(bf16[4,96,3072]{2,1,0:T(8,128)(2,1)} %bitcast.69), calls=%async_computation.2 | async-start | bytes 4718592 | tf_op jit(solution)/shard_map/all_to_all | solution.py:60
  30.6 36.1 %all-gather.7.cloned.1.call-start = ((), (), s32[]{:S(2)}) async-start(), calls=%async_computation.10 | async-start | bytes 2359296 | tf_op jit(solution)/shard_map/all_gather | solution.py:53
  58.8 32.0 %all-to-all-start.1 = ((bf16[4,96,3072]{2,1,0:T(8,128)(2,1)}), bf16[4,96,3072]{2,1,0:T(8,128)(2,1)}, u32[]{:S(2)}, u32[]{:S(2)}) async-start(bf16[4,96,3072]{2,1,0:T(8,128)(2,1)} %bitcast.68), calls=%async_computation.1 | async-start | bytes 4718592 | tf_op jit(solution)/shard_map/all_to_all | solution.py:61
  63.3 21.1 %all-gather.5.cloned.1.call-start = ((), (), s32[]{:S(2)}) async-start(), calls=%async_computation.9 | async-start | bytes 2359296 | tf_op jit(solution)/shard_map/all_gather | solution.py:54
  64.0 191.3 %all-reduce.7.cloned.1.call-start = ((), (), s32[]{:S(2)}) async-start(), calls=%async_computation.16 | async-start | bytes 4718592
  90.7 4.1 %copy-start = (bf16[1,3072,256]{2,1,0:T(8,128)(2,1)S(1)}, bf16[1,3072,256]{2,1,0:T(8,128)(2,1)}, u32[]{:S(2)}) copy-start(bf16[1,3072,256]{2,1,0:T(8,128)(2,1)} %all-gather.9.cloned.1.call-done) | copy-start | bytes 4718596
  94.8 1.4 copy-start.1
  100.3 0.7 copy-start.3
  100.3 156.7 %copy-start.4 = (bf16[384,256]{0,1:T(8,128)(2,1)S(1)}, bf16[384,256]{0,1:T(8,128)(2,1)}, u32[]{:S(2)}) copy-start(bf16[384,256]{0,1:T(8,128)(2,1)} %get-tuple-element.21) | copy-start | bytes 589828
  100.3 257.8 %all-gather.11.cloned.1.call-start = ((), (), s32[]{:S(2)}) async-start(), calls=%async_computation.12 | async-start | bytes 2433024 | tf_op jit(solution)/shard_map/all_gather | solution.py:101
  256.9 139.5 %reduce-scatter.9.cloned.1.call-start = ((), (), s32[]{:S(2)}) async-start(), calls=%async_computation.15 | async-start | bytes 2359296 | tf_op jit(solution)/shard_map/reduce_scatter | solution.py:118
  261.0 135.4 %reduce-scatter.7.cloned.1.call-start = ((), (), s32[]{:S(2)}) async-start(), calls=%async_computation.14 | async-start | bytes 2359296 | tf_op jit(solution)/shard_map/reduce_scatter | solution.py:115
  263.3 133.1 %reduce-scatter.5.cloned.1.call-start = ((), (), s32[]{:S(2)}) async-start(), calls=%async_computation.13 | async-start | bytes 2359296 | tf_op jit(solution)/shard_map/reduce_scatter | solution.py:112
  353.8 9.5 %all-to-all-start.5 = ((bf16[4,1,96]{2,1,0:T(2,128)(2,1)}), bf16[4,1,96]{2,1,0:T(2,128)(2,1)S(1)}, u32[]{:S(2)}, u32[]{:S(2)}) async-start(bf16[4,1,96]{2,1,0:T(2,128)(2,1)} %all_to_all.33), calls=%async_computation.5 | async-start | bytes 4096 | tf_op jit(solution)/shard_map/all_to_all | solution.py:106
  363.4 21.7 %all-to-all-start.3 = ((bf16[4,96,3072]{2,1,0:T(8,128)(2,1)}), bf16[4,96,3072]{2,1,0:T(8,128)(2,1)S(1)}, u32[]{:S(2)}, u32[]{:S(2)}) async-start(bf16[4,96,3072]{2,1,0:T(8,128)(2,1)} %copy.41), calls=%async_computation.3 | async-start | bytes 4718592 | tf_op jit(solution)/shard_map/all_to_all | solution.py:105
Sparse Core Ops, SparseCore 0:
  9.8 18.0 all-gather.8
  33.2 18.4 all-gather.6
  65.9 18.4 all-gather.4
  100.5 154.8 all-reduce.6
  258.4 75.9 all-gather.10
  337.3 13.0 reduce-scatter.8
  353.4 15.7 reduce-scatter.6
  372.3 15.7 reduce-scatter.4
